TPU v7x, 32 devices: a whole 2x2x4 slice. The times are simulated.
32 devices in a mesh: energy: 2 (over x), chain: 16 (over z, y, core).
Axes of the slice: x: 2, y: 2, z: 4, core: 2. Of those that a mesh axis runs over, the one named last changes fastest.
Arguments:
- lower: bfloat16 [32, 2, 256, 256], P(('energy', 'chain')), parts along dimension 0, may hold values from -0.125 to 0.125
- upper: bfloat16 [32, 2, 256, 256], P(('energy', 'chain')), parts along dimension 0, may hold values from -0.125 to 0.125
- right_side: bfloat16 [32, 2, 256, 256], P(('energy', 'chain')), parts along dimension 0, may hold values from -6 to 6
Outputs:
- reduced_rhs: bfloat16 [32, 2, 256, 256], P(('energy', 'chain')), parts along dimension 0
There are 2 independent parts, one for each index of `energy`. A program takes and returns all parts, laid end to end along the dimension named above; each array names one. Nothing has to cross between parts.
All inputs are finite; a program needn't handle non-finite values.
Results may differ from a plain program's by a relative error of at most 0.011.
Values may be sent and summed in bfloat16 or wider, within the bound.
A program may use at most 64 MiB of HBM per device.

v0:
```python
import jax
import jax.numpy as jnp
from jax import lax
from jax.sharding import PartitionSpec as P

SECTIONS = 3
NS_STEPS = 2


def passed_along(shard, axis, by):
    length = lax.axis_size(axis)
    pairs = [(i, i + by) for i in range(length) if 0 <= i + by < length]
    return lax.ppermute(shard, axis, pairs)


def complex_product(left_block, right_block):
    real_part = jnp.dot(
        left_block[0], right_block[0], preferred_element_type=jnp.float32
    ) - jnp.dot(left_block[1], right_block[1], preferred_element_type=jnp.float32)
    imag_part = jnp.dot(
        left_block[0], right_block[1], preferred_element_type=jnp.float32
    ) + jnp.dot(left_block[1], right_block[0], preferred_element_type=jnp.float32)
    return jnp.stack([real_part, imag_part])


def approx_inverse(diagonal_new, identity_block):
    diagonal_low = diagonal_new.astype(jnp.bfloat16)
    approx = (2.0 * identity_block - diagonal_new).astype(jnp.bfloat16)
    for repeat in range(NS_STEPS):
        correction = (2.0 * identity_block - complex_product(diagonal_low, approx)).astype(
            jnp.bfloat16
        )
        approx = complex_product(approx, correction).astype(jnp.bfloat16)
    return approx


def exchange_rows(send_upward, send_downward, reach):
    below = passed_along(send_upward, "chain", reach)[0]
    above = passed_along(send_downward, "chain", -reach)[0]
    return (below, above)


def local(lower, upper, right_side):
    order = lower.shape[2]
    lower_block = lower[0]
    upper_block = upper[0]
    current = right_side[0]
    unit_matrix = jnp.eye(order, dtype=jnp.float32)
    identity_block = jnp.stack([unit_matrix, jnp.zeros_like(unit_matrix)])
    for number in range(SECTIONS):
        reach = 2**number
        final = number == SECTIONS - 1
        if final:
            send_upward = jnp.concatenate([upper_block, current], axis=-1)[None]
            send_downward = jnp.concatenate([lower_block, current], axis=-1)[None]
            below, above = exchange_rows(send_upward, send_downward, reach)
            below_upper = below[:, :, :order]
            below_rhs = below[:, :, order:]
            above_lower = above[:, :, :order]
            above_rhs = above[:, :, order:]
        else:
            packed = jnp.concatenate([lower_block, upper_block, current], axis=-1)[None]
            below, above = exchange_rows(packed, packed, reach)
            below_lower = below[:, :, :order]
            below_upper = below[:, :, order : 2 * order]
            below_rhs = below[:, :, 2 * order :]
            above_lower = above[:, :, :order]
            above_upper = above[:, :, order : 2 * order]
            above_rhs = above[:, :, 2 * order :]
        diagonal_new = (
            identity_block
            - complex_product(lower_block, below_upper)
            - complex_product(upper_block, above_lower)
        )
        inverse = approx_inverse(diagonal_new, identity_block)
        rhs_new = (
            current
            - complex_product(lower_block, below_rhs)
            - complex_product(upper_block, above_rhs)
        ).astype(jnp.bfloat16)
        if not final:
            lower_raw = (-complex_product(lower_block, below_lower)).astype(jnp.bfloat16)
            upper_raw = (-complex_product(upper_block, above_upper)).astype(jnp.bfloat16)
            lower_block = complex_product(inverse, lower_raw).astype(jnp.bfloat16)
            upper_block = complex_product(inverse, upper_raw).astype(jnp.bfloat16)
        current = complex_product(inverse, rhs_new).astype(jnp.bfloat16)
    return current[None]


def solution(mesh):
    placed = (
        P(("energy", "chain"), None, None, None),
        P(("energy", "chain"), None, None, None),
        P(("energy", "chain"), None, None, None),
    )
    return jax.shard_map(
        local,
        mesh=mesh,
        in_specs=placed,
        out_specs=P(("energy", "chain"), None, None, None),
        check_vma=False,
    )
```

profile of v0, /device:TPU:0, one launch (start us, length us, event | category | flops | bytes accessed | tf_op | source)
XLA Modules:
  0.0 114.5 jit_solution(17838638921217624509)
XLA Ops:
  0.0 1.1 copy.6
  1.1 1.1 copy.4
  2.4 1.3 %collective-permute-start.1 = (bf16[1,2,256,768]{2,3,1,0:T(8,128)(2,1)S(1)}, bf16[1,2,256,768]{2,3,1,0:T(8,128)(2,1)S(1)}, u32[]{:S(2)}, u32[]{:S(2)}) collective-permute-start(bf16[1,2,256,768]{2,3,1,0:T(8,128)(2,1)S(1)} %maximum_bitcast_fusion), channel_id=1, source_target_pairs={{1,0},{2,1},{3,2},{4,3},{5,4},{6,5},{7,6},{8,7},{9,8},{10,9},{11,1... | collective-permute-start | bytes 2359304 | tf_op jit(solution)/shard_map/ppermute | solution.py:13
  3.7 3.1 %collective-permute-start = (bf16[1,2,256,768]{2,3,1,0:T(8,128)(2,1)S(1)}, bf16[1,2,256,768]{2,3,1,0:T(8,128)(2,1)S(1)}, u32[]{:S(2)}, u32[]{:S(2)}) collective-permute-start(bf16[1,2,256,768]{2,3,1,0:T(8,128)(2,1)S(1)} %maximum_bitcast_fusion), channel_id=1, source_target_pairs={{0,1},{1,2},{2,3},{3,4},{4,5},{5,6},{6,7},{7,8},{8,9},{9,10},{10,1... | collective-permute-start | bytes 2359304 | tf_op jit(solution)/shard_map/ppermute | solution.py:13
  8.2 0.4 collective-permute-done
  13.3 0.2 fusion.38
  13.5 0.2 fusion.39
  19.5 1.3 %collective-permute-start.3 = (bf16[1,2,256,768]{2,3,1,0:T(8,128)(2,1)S(1)}, bf16[1,2,256,768]{2,3,1,0:T(8,128)(2,1)S(1)}, u32[]{:S(2)}, u32[]{:S(2)}) collective-permute-start(bf16[1,2,256,768]{2,3,1,0:T(8,128)(2,1)S(1)} %maximum_bitcast_fusion.1), channel_id=1, source_target_pairs={{2,0},{3,1},{4,2},{5,3},{6,4},{7,5},{8,6},{9,7},{10,8},{11,9},{12,... | collective-permute-start | bytes 2359304 | tf_op jit(solution)/shard_map/ppermute | solution.py:13
  20.8 22.0 %collective-permute-start.2 = (bf16[1,2,256,768]{2,3,1,0:T(8,128)(2,1)S(1)}, bf16[1,2,256,768]{2,3,1,0:T(8,128)(2,1)S(1)}, u32[]{:S(2)}, u32[]{:S(2)}) collective-permute-start(bf16[1,2,256,768]{2,3,1,0:T(8,128)(2,1)S(1)} %maximum_bitcast_fusion.1), channel_id=1, source_target_pairs={{0,2},{1,3},{2,4},{3,5},{4,6},{5,7},{6,8},{7,9},{8,10},{9,11},{10,... | collective-permute-start | bytes 2359304 | tf_op jit(solution)/shard_map/ppermute | solution.py:13
  42.8 15.1 %collective-permute-done.3 = bf16[1,2,256,768]{2,3,1,0:T(8,128)(2,1)S(1)} collective-permute-done((bf16[1,2,256,768]{2,3,1,0:T(8,128)(2,1)S(1)}, bf16[1,2,256,768]{2,3,1,0:T(8,128)(2,1)S(1)}, u32[]{:S(2)}, u32[]{:S(2)}) %collective-permute-start.3) | collective-permute-done | bytes 786464 | tf_op jit(solution)/shard_map/ppermute | solution.py:13
  59.1 15.9 %collective-permute-done.2 = bf16[1,2,256,768]{2,3,1,0:T(8,128)(2,1)S(1)} collective-permute-done((bf16[1,2,256,768]{2,3,1,0:T(8,128)(2,1)S(1)}, bf16[1,2,256,768]{2,3,1,0:T(8,128)(2,1)S(1)}, u32[]{:S(2)}, u32[]{:S(2)}) %collective-permute-start.2) | collective-permute-done | bytes 786464 | tf_op jit(solution)/shard_map/ppermute | solution.py:13
  79.3 0.2 fusion.28
  79.6 0.2 fusion.29
  83.3 0.2 fusion.166
  83.6 0.2 fusion.165
  84.0 0.2 fusion.63
  84.7 0.2 fusion.60
  85.0 0.2 fusion.59
  85.2 0.2 fusion.58
  85.5 5.6 %collective-permute-start.4 = (bf16[1,2,256,512]{2,3,1,0:T(8,128)(2,1)S(1)}, bf16[1,2,256,512]{2,3,1,0:T(8,128)(2,1)S(1)}, u32[]{:S(2)}, u32[]{:S(2)}) collective-permute-start(bf16[1,2,256,512]{2,3,1,0:T(8,128)(2,1)S(1)} %get-tuple-element.11), channel_id=1, source_target_pairs={{0,4},{1,5},{2,6},{3,7},{4,8},{5,9},{6,10},{7,11},{8,12},{9,13},{1... | collective-permute-start | bytes 1572872 | tf_op jit(solution)/shard_map/ppermute | solution.py:13
  91.2 1.5 %collective-permute-start.5 = (bf16[1,2,256,512]{2,3,1,0:T(8,128)(2,1)S(1)}, bf16[1,2,256,512]{2,3,1,0:T(8,128)(2,1)S(1)}, u32[]{:S(2)}, u32[]{:S(2)}) collective-permute-start(bf16[1,2,256,512]{2,3,1,0:T(8,128)(2,1)S(1)} %get-tuple-element.12), channel_id=1, source_target_pairs={{4,0},{5,1},{6,2},{7,3},{8,4},{9,5},{10,6},{11,7},{12,8},{13,9},{1... | collective-permute-start | bytes 1572872 | tf_op jit(solution)/shard_map/ppermute | solution.py:13
  92.6 9.9 %collective-permute-done.4 = bf16[1,2,256,512]{2,3,1,0:T(8,128)(2,1)S(1)} collective-permute-done((bf16[1,2,256,512]{2,3,1,0:T(8,128)(2,1)S(1)}, bf16[1,2,256,512]{2,3,1,0:T(8,128)(2,1)S(1)}, u32[]{:S(2)}, u32[]{:S(2)}) %collective-permute-start.4) | collective-permute-done | bytes 524320 | tf_op jit(solution)/shard_map/ppermute | solution.py:13
  103.3 3.4 %collective-permute-done.5 = bf16[1,2,256,512]{2,3,1,0:T(8,128)(2,1)S(1)} collective-permute-done((bf16[1,2,256,512]{2,3,1,0:T(8,128)(2,1)S(1)}, bf16[1,2,256,512]{2,3,1,0:T(8,128)(2,1)S(1)}, u32[]{:S(2)}, u32[]{:S(2)}) %collective-permute-start.5) | collective-permute-done | bytes 524320 | tf_op jit(solution)/shard_map/ppermute | solution.py:13
  113.8 0.7 pad_maximum_fusion.1
  (156 shorter events, 28.5 us)
Async XLA Ops:
  0.0 2.2 %copy-start = (bf16[1,2,256,256]{3,2,1,0:T(8,128)(2,1)S(1)}, bf16[1,2,256,256]{3,2,1,0:T(8,128)(2,1)}, u32[]{:S(2)}) copy-start(bf16[1,2,256,256]{3,2,1,0:T(8,128)(2,1)} %param.4) | copy-start | bytes 786436
  2.4 4.4 %collective-permute-start.1 = (bf16[1,2,256,768]{2,3,1,0:T(8,128)(2,1)S(1)}, bf16[1,2,256,768]{2,3,1,0:T(8,128)(2,1)S(1)}, u32[]{:S(2)}, u32[]{:S(2)}) collective-permute-start(bf16[1,2,256,768]{2,3,1,0:T(8,128)(2,1)S(1)} %maximum_bitcast_fusion), channel_id=1, source_target_pairs={{1,0},{2,1},{3,2},{4,3},{5,4},{6,5},{7,6},{8,7},{9,8},{10,9},{11,1... | collective-permute-start | bytes 2359304 | tf_op jit(solution)/shard_map/ppermute | solution.py:13
  3.7 4.9 %collective-permute-start = (bf16[1,2,256,768]{2,3,1,0:T(8,128)(2,1)S(1)}, bf16[1,2,256,768]{2,3,1,0:T(8,128)(2,1)S(1)}, u32[]{:S(2)}, u32[]{:S(2)}) collective-permute-start(bf16[1,2,256,768]{2,3,1,0:T(8,128)(2,1)S(1)} %maximum_bitcast_fusion), channel_id=1, source_target_pairs={{0,1},{1,2},{2,3},{3,4},{4,5},{5,6},{6,7},{7,8},{8,9},{9,10},{10,1... | collective-permute-start | bytes 2359304 | tf_op jit(solution)/shard_map/ppermute | solution.py:13
  7.5 1.1 copy-start.1
  19.5 38.4 %collective-permute-start.3 = (bf16[1,2,256,768]{2,3,1,0:T(8,128)(2,1)S(1)}, bf16[1,2,256,768]{2,3,1,0:T(8,128)(2,1)S(1)}, u32[]{:S(2)}, u32[]{:S(2)}) collective-permute-start(bf16[1,2,256,768]{2,3,1,0:T(8,128)(2,1)S(1)} %maximum_bitcast_fusion.1), channel_id=1, source_target_pairs={{2,0},{3,1},{4,2},{5,3},{6,4},{7,5},{8,6},{9,7},{10,8},{11,9},{12,... | collective-permute-start | bytes 2359304 | tf_op jit(solution)/shard_map/ppermute | solution.py:13
  20.8 54.2 %collective-permute-start.2 = (bf16[1,2,256,768]{2,3,1,0:T(8,128)(2,1)S(1)}, bf16[1,2,256,768]{2,3,1,0:T(8,128)(2,1)S(1)}, u32[]{:S(2)}, u32[]{:S(2)}) collective-permute-start(bf16[1,2,256,768]{2,3,1,0:T(8,128)(2,1)S(1)} %maximum_bitcast_fusion.1), channel_id=1, source_target_pairs={{0,2},{1,3},{2,4},{3,5},{4,6},{5,7},{6,8},{7,9},{8,10},{9,11},{10,... | collective-permute-start | bytes 2359304 | tf_op jit(solution)/shard_map/ppermute | solution.py:13
  85.5 17.1 %collective-permute-start.4 = (bf16[1,2,256,512]{2,3,1,0:T(8,128)(2,1)S(1)}, bf16[1,2,256,512]{2,3,1,0:T(8,128)(2,1)S(1)}, u32[]{:S(2)}, u32[]{:S(2)}) collective-permute-start(bf16[1,2,256,512]{2,3,1,0:T(8,128)(2,1)S(1)} %get-tuple-element.11), channel_id=1, source_target_pairs={{0,4},{1,5},{2,6},{3,7},{4,8},{5,9},{6,10},{7,11},{8,12},{9,13},{1... | collective-permute-start | bytes 1572872 | tf_op jit(solution)/shard_map/ppermute | solution.py:13
  91.2 15.6 %collective-permute-start.5 = (bf16[1,2,256,512]{2,3,1,0:T(8,128)(2,1)S(1)}, bf16[1,2,256,512]{2,3,1,0:T(8,128)(2,1)S(1)}, u32[]{:S(2)}, u32[]{:S(2)}) collective-permute-start(bf16[1,2,256,512]{2,3,1,0:T(8,128)(2,1)S(1)} %get-tuple-element.12), channel_id=1, source_target_pairs={{4,0},{5,1},{6,2},{7,3},{8,4},{9,5},{10,6},{11,7},{12,8},{13,9},{1... | collective-permute-start | bytes 1572872 | tf_op jit(solution)/shard_map/ppermute | solution.py:13
where the time goes:
time: 115 us
  waiting for transfers between devices  44.8 us (39%)
  starting transfers between devices  34.8 us (30%)
  matrix products  29.3 us (25%)
  local copies, waits for them, and re-layouts  2.35 us (2%)
  other arithmetic  2.09 us (2%)
  between operations  1.22 us (1%)
    ppermute x6, waiting for transfers between devices, passed_along(): return lax.ppermute(shard, axis, pairs)  44.8 us
    ppermute x6, starting transfers between devices, passed_along(): return lax.ppermute(shard, axis, pairs)  34.8 us
    dot_general x35, matrix products, complex_product(): jnp.dot(left_block[1], right_block[0], preferred_element_type=jnp.float32)  7.34 us
    dot_general x35, matrix products, complex_product(): jnp.dot(left_block[1], right_block[1], preferred_element_type=jnp.float32)  7.33 us
    dot_general x35, matrix products, complex_product(): jnp.dot(left_block[0], right_block[0], preferred_element_type=jnp.float32)  7.33 us
    dot_general x35, matrix products, complex_product(): jnp.dot(left_block[0], right_block[1], preferred_element_type=jnp.float32)  7.32 us
    unnamed x7, local copies, waits for them, and re-layouts  2.35 us
  transfers between devices with their start and end apart: 6, of which 5 were waited for; matrix products, arithmetic and copies ran while one was open for 3% of the time, Pallas kernels for 0%

commit v1 on v0

v1 whole, which is shorter than its diff:
```python
import functools

import jax
import jax.numpy as jnp
from jax import lax
from jax.experimental import pallas as pl
from jax.experimental.pallas import tpu as pltpu
from jax.sharding import PartitionSpec as P

NS_STEPS = 2
MESH = pl.DeviceIdType.MESH
RHS = 2


def product(left, right):
    order = left.shape[1]
    tall = left.reshape(2 * order, left.shape[2])
    by_real = jnp.dot(tall, right[0], preferred_element_type=jnp.float32)
    by_imag = jnp.dot(tall, right[1], preferred_element_type=jnp.float32)
    return by_real[:order] - by_imag[order:], by_imag[:order] + by_real[order:]


def rounded(parts):
    return jnp.stack([parts[0].astype(jnp.bfloat16), parts[1].astype(jnp.bfloat16)])


def kernel(
    quads, l_ref, u_ref, b_ref, out_ref,
    buf, new1, got1, new2, got2, last, mid,
    sem_home, sem_buf, sem_send0, sem_relay, sem_got1, sem_send1, sem_got2, sem_send2, sem_out,
):
    me = lax.axis_index("chain")
    q = me // 4
    a = (me // 2) % 2
    b = me % 2
    inner = a != b
    outer = a == b
    f = 1 - a
    g = a
    cf = 2 - a
    cg = 1 + a

    def at(quad, y, core):
        return {"chain": quad * 4 + y * 2 + core}

    mate = at(q, a, 1 - b)
    across = at(q, 1 - a, b)
    twin = at(q, b, a)
    up1, has_up1 = at(q + b, a, 1 - b), q + b < quads
    down1, has_down1 = at(q - 1 + b, a, 1 - b), q - 1 + b >= 0
    up2, has_up2 = at(q + 1, a, b), q + 1 < quads
    down2, has_down2 = at(q - 1, a, b), q >= 1
    far_step = 2 * b - 1
    far, has_far = at(q + far_step, a, 1 - b), (q + far_step >= 0) & (q + far_step < quads)
    inputs = (l_ref, u_ref, b_ref)

    home_slot = jnp.where(inner, 1 + a, 0)
    for u in range(3):
        pltpu.make_async_copy(inputs[u].at[0], buf.at[home_slot, u], sem_home.at[u]).start()

    barrier = pltpu.get_barrier_semaphore()

    def greet(who):
        pl.semaphore_signal(barrier, inc=1, device_id=who, device_id_type=MESH)

    greet(mate)
    greet(across)
    for exists, who in ((inner, twin), (has_far, far), (has_up2, up2), (has_down2, down2)):
        pl.when(exists)(functools.partial(greet, who))
    count = (
        2
        + inner.astype(jnp.int32)
        + has_far.astype(jnp.int32)
        + has_up2.astype(jnp.int32)
        + has_down2.astype(jnp.int32)
    )
    pl.semaphore_wait(barrier, count)

    def remote(src, dst, send, recv, who):
        return pltpu.make_async_remote_copy(
            src_ref=src, dst_ref=dst, send_sem=send, recv_sem=recv,
            device_id=who, device_id_type=MESH,
        )

    def send0(u, which, slot, who, half, order_u):
        return remote(
            inputs[u].at[0, half],
            buf.at[slot, u, half],
            sem_send0.at[which, u, half],
            sem_buf.at[slot, u, half],
            who,
        )

    def over_y(u, half):
        who = {"chain": jnp.where(inner, twin["chain"], across["chain"])}
        return send0(u, 0, jnp.where(inner, 0, 1 + a), who, half, None)

    def to_mate(u, half):
        return send0(u, 1, 2 - a, mate, half, None)

    def both_orders(start):
        @pl.when(a == 1)
        def _():
            for u in (0, 1, 2):
                start(u)

        @pl.when(a == 0)
        def _():
            for u in (1, 0, 2):
                start(u)

    def start_y(u):
        for half in range(2):
            over_y(u, half).start()

    both_orders(start_y)

    @pl.when(inner)
    def _():
        for u in range(3):
            for half in range(2):
                to_mate(u, half).start()

    none_far0 = outer & jnp.logical_not(has_far)
    zeros3 = jnp.zeros(buf.shape[1:], jnp.bfloat16)
    zeros2 = jnp.zeros(got2.shape[1:], jnp.bfloat16)

    @pl.when(none_far0)
    def _():
        buf[1 + a] = zeros3

    @pl.when(jnp.logical_not(has_down1))
    def _():
        got1[0] = zeros3

    @pl.when(jnp.logical_not(has_up1))
    def _():
        got1[1] = zeros3

    @pl.when(jnp.logical_not(has_down2))
    def _():
        got2[0] = zeros2

    @pl.when(jnp.logical_not(has_up2))
    def _():
        got2[1] = zeros2

    def arrive(ref, sem):
        pltpu.make_async_copy(ref, ref, sem).wait()

    def wait_home(u):
        pltpu.make_async_copy(inputs[u].at[0], buf.at[home_slot, u], sem_home.at[u]).wait()

    for u in range(3):
        wait_home(u)

    def relay(u, half):
        return remote(
            buf.at[2 - a, u, half],
            buf.at[1 + a, u, half],
            sem_relay.at[u, half],
            sem_buf.at[1 + a, u, half],
            far,
        )

    def wait_unit(u):
        for half in range(2):
            @pl.when(inner)
            def _():
                arrive(buf.at[2 - a, u, half], sem_buf.at[2 - a, u, half])

                @pl.when(has_far)
                def _():
                    relay(u, half).start()

        @pl.when(inner)
        def _():
            for half in range(2):
                arrive(buf.at[0, u, half], sem_buf.at[0, u, half])

        @pl.when(outer)
        def _():
            for half in range(2):
                arrive(buf.at[2 - a, u, half], sem_buf.at[2 - a, u, half])

    def wait_far(u):
        @pl.when(outer & has_far)
        def _():
            for half in range(2):
                arrive(buf.at[1 + a, u, half], sem_buf.at[1 + a, u, half])

    order = out_ref.shape[-1]
    row = lax.broadcasted_iota(jnp.int32, (l_ref.shape[2], l_ref.shape[3]), 0)
    col = lax.broadcasted_iota(jnp.int32, (l_ref.shape[2], l_ref.shape[3]), 1)
    unit = (row == col).astype(jnp.float32)
    del order

    def inverse(diag):
        low = rounded(diag)
        approx = rounded((2.0 * unit - diag[0], -diag[1]))
        for _ in range(NS_STEPS):
            prod = product(low, approx)
            fix = rounded((2.0 * unit - prod[0], -prod[1]))
            approx = rounded(product(approx, fix))
        return approx

    def negated(parts):
        return -parts[0], -parts[1]

    def diagonal(one, two):
        return unit - one[0] - two[0], -one[1] - two[1]

    def rhs(own, one, two):
        return rounded(
            (
                own[0].astype(jnp.float32) - one[0] - two[0],
                own[1].astype(jnp.float32) - one[1] - two[1],
            )
        )

    def send1(u, to_up):
        side = 0 if to_up else 1
        return remote(
            new1.at[u], got1.at[side, u], sem_send1.at[side, u], sem_got1.at[side, u],
            up1 if to_up else down1,
        )

    def start1(u):
        pl.when(has_up1)(lambda: send1(u, True).start())
        pl.when(has_down1)(lambda: send1(u, False).start())

    wait_unit(f)
    mid[0] = rounded(negated(product(buf[0, f], buf[cf, f])))
    wait_unit(g)
    wait_far(f)
    x = inverse(
        diagonal(product(buf[0, f], buf[cf, g]), product(buf[0, g], buf[cg, f]))
    )
    mid[2] = x
    new1[f] = rounded(product(x, mid[0]))
    start1(f)
    wait_far(g)
    mid[1] = rounded(negated(product(buf[0, g], buf[cg, g])))
    new1[g] = rounded(product(mid[2], mid[1]))
    start1(g)
    wait_unit(RHS)
    one = product(buf[0, f], buf[cf, RHS])
    wait_far(RHS)
    two = product(buf[0, g], buf[cg, RHS])
    new1[RHS] = rounded(product(mid[2], rhs(buf[0, RHS], one, two)))
    start1(RHS)

    def wait1(u):
        @pl.when(has_down1)
        def _():
            arrive(got1.at[0, u], sem_got1.at[0, u])

        @pl.when(has_up1)
        def _():
            arrive(got1.at[1, u], sem_got1.at[1, u])

    def send2(u, to_up):
        side = 0 if to_up else 1
        place = 1 if u is RHS else 0
        return remote(
            new2.at[u], got2.at[side, place], sem_send2.at[side, place],
            sem_got2.at[side, place], up2 if to_up else down2,
        )

    ef, eg = cf - 1, cg - 1
    wait1(f)
    mid[0] = rounded(negated(product(new1[f], got1[ef, f])))
    wait1(g)
    x = inverse(
        diagonal(product(new1[f], got1[ef, g]), product(new1[g], got1[eg, f]))
    )
    mid[2] = x
    new2[f] = rounded(product(x, mid[0]))

    def start2(is_upper):
        @pl.when(has_up2 & is_upper)
        def _():
            send2(1, True).start()

        @pl.when(has_down2 & jnp.logical_not(is_upper))
        def _():
            send2(0, False).start()

    start2(f == 1)
    mid[1] = rounded(negated(product(new1[g], got1[eg, g])))
    new2[g] = rounded(product(mid[2], mid[1]))
    start2(g == 1)
    wait1(RHS)
    one = product(new1[f], got1[ef, RHS])
    two = product(new1[g], got1[eg, RHS])
    new2[RHS] = rounded(product(mid[2], rhs(new1[RHS], one, two)))
    pl.when(has_up2)(lambda: send2(RHS, True).start())
    pl.when(has_down2)(lambda: send2(RHS, False).start())

    def wait2(place):
        @pl.when(has_down2)
        def _():
            arrive(got2.at[0, place], sem_got2.at[0, place])

        @pl.when(has_up2)
        def _():
            arrive(got2.at[1, place], sem_got2.at[1, place])

    wait2(0)
    x = inverse(
        diagonal(product(new2[0], got2[0, 0]), product(new2[1], got2[1, 0]))
    )
    mid[2] = x
    wait2(1)
    one = product(new2[0], got2[0, 1])
    two = product(new2[1], got2[1, 1])
    last[...] = rounded(product(mid[2], rhs(new2[RHS], one, two)))

    def home():
        return remote(last, out_ref.at[0], sem_out.at[0], sem_out.at[1], twin)

    def keep():
        return pltpu.make_async_copy(last, out_ref.at[0], sem_out.at[1])

    pl.when(inner)(lambda: home().start())
    pl.when(outer)(lambda: keep().start())

    for u in range(3):
        for half in range(2):
            over_y(u, half).wait_send()

            @pl.when(inner)
            def _(u=u, half=half):
                to_mate(u, half).wait_send()

            @pl.when(inner & has_far)
            def _(u=u, half=half):
                relay(u, half).wait_send()

        pl.when(has_up1)(lambda u=u: send1(u, True).wait_send())
        pl.when(has_down1)(lambda u=u: send1(u, False).wait_send())
    for u in (1, RHS):
        pl.when(has_up2)(lambda u=u: send2(u, True).wait_send())
    for u in (0, RHS):
        pl.when(has_down2)(lambda u=u: send2(u, False).wait_send())

    @pl.when(inner)
    def _():
        home().wait()

    pl.when(outer)(lambda: keep().wait())


def local(quads, lower, upper, right_side):
    block = lower.shape[1:]
    any_spec = pl.BlockSpec(memory_space=pl.ANY)
    low = jnp.bfloat16
    dma = pltpu.SemaphoreType.DMA
    return pl.pallas_call(
        functools.partial(kernel, quads),
        out_shape=jax.ShapeDtypeStruct(right_side.shape, right_side.dtype),
        in_specs=[any_spec] * 3,
        out_specs=any_spec,
        scratch_shapes=[
            pltpu.VMEM((3, 3, *block), low),
            pltpu.VMEM((3, *block), low),
            pltpu.VMEM((2, 3, *block), low),
            pltpu.VMEM((3, *block), low),
            pltpu.VMEM((2, 2, *block), low),
            pltpu.VMEM(block, low),
            pltpu.VMEM((3, *block), low),
            dma((3,)),
            dma((3, 3, 2)),
            dma((2, 3, 2)),
            dma((3, 2)),
            dma((2, 3)),
            dma((2, 3)),
            dma((2, 2)),
            dma((2, 2)),
            dma((2,)),
        ],
        compiler_params=pltpu.CompilerParams(collective_id=0, has_side_effects=True),
    )(lower, upper, right_side)


def solution(mesh):
    placed = P(("energy", "chain"), None, None, None)
    return jax.shard_map(
        functools.partial(local, mesh.shape["chain"] // 4),
        mesh=mesh,
        in_specs=(placed,) * 3,
        out_specs=placed,
        check_vma=False,
    )
```

time: 115 us -> 57.6 us (0.50)
  the two profiles are of different devices: /device:TPU:0 before, /device:TPU:11 now
where the time goes in v1:
time: 57.6 us; the launch traced here: 56.7 us
  Pallas kernels  55 us (95%)
  local copies, waits for them, and re-layouts  1.67 us (3%)
    pallas_call x1, Pallas kernels, local(): pl.pallas_call(functools.partial(kernel, quads), out_shape=jax.ShapeDtype...  55 us
    unnamed x1, local copies, waits for them, and re-layouts  1.67 us

profile of v1, /device:TPU:11, one launch (start us, length us, event | category | flops | bytes accessed | tf_op | source)
XLA Modules:
  0.0 56.7 jit_solution(7057713087825336670)
XLA Ops:
  0.0 55.0 %shard_map.37 = bf16[1,2,256,256]{3,2,1,0:T(8,128)(2,1)} custom-call(bf16[1,2,256,256]{3,2,1,0:T(8,128)(2,1)} %l_ref.1, bf16[1,2,256,256]{3,2,1,0:T(8,128)(2,1)} %u_ref.1, bf16[1,2,256,256]{3,2,1,0:T(8,128)(2,1)} %b_ref.1), custom_call_target="tpu_custom_call" | custom-call | tf_op jit(solution)/shard_map/pallas_call | solution.py:359
  55.0 1.7 %copy.5 = bf16[1,2,256,256]{3,2,1,0:T(8,128)(2,1)} copy(bf16[1,2,256,256]{3,2,1,0:T(8,128)(2,1)} %shard_map.37) | data formatting | bytes 524288

commit v2 on v1

v2 whole, which is shorter than its diff:
```python
import functools

import jax
import jax.numpy as jnp
from jax import lax
from jax.experimental import pallas as pl
from jax.experimental.pallas import tpu as pltpu
from jax.sharding import PartitionSpec as P

NS_STEPS = 2
MESH = pl.DeviceIdType.MESH
RHS = 2


def is_rhs(u):
    return isinstance(u, int) and u >= RHS


def product(left, right):
    order = left.shape[1]
    tall = left.reshape(2 * order, left.shape[2])
    by_real = jnp.dot(tall, right[0], preferred_element_type=jnp.float32)
    by_imag = jnp.dot(tall, right[1], preferred_element_type=jnp.float32)
    return by_real[:order] - by_imag[order:], by_imag[:order] + by_real[order:]


def rounded(parts):
    return jnp.stack([parts[0].astype(jnp.bfloat16), parts[1].astype(jnp.bfloat16)])


def kernel(
    quads, l_ref, u_ref, b_ref, out_ref,
    buf, bbuf, new1, nb1, got1, gb1, new2, nb2, got2, gb2, last, mid,
    sem_home, sem_bhome, sem_buf, sem_send0, sem_relay,
    sem_got1, sem_send1, sem_got2, sem_send2, sem_out,
):
    me = lax.axis_index("chain")
    q = me // 4
    a = (me // 2) % 2
    b = me % 2
    inner = a != b
    outer = a == b
    f = 1 - a
    g = a
    cf = 2 - a
    cg = 1 + a

    def at(quad, y, core):
        return {"chain": quad * 4 + y * 2 + core}

    mate = at(q, a, 1 - b)
    across = at(q, 1 - a, b)
    twin = at(q, b, a)
    up1, has_up1 = at(q + b, a, 1 - b), q + b < quads
    down1, has_down1 = at(q - 1 + b, a, 1 - b), q - 1 + b >= 0
    up2, has_up2 = at(q + 1, a, b), q + 1 < quads
    down2, has_down2 = at(q - 1, a, b), q >= 1
    far_step = 2 * b - 1
    far, has_far = at(q + far_step, a, 1 - b), (q + far_step >= 0) & (q + far_step < quads)
    inputs = (l_ref, u_ref)
    wide = b_ref.shape[3] // 2

    def place0(slot, u, half):
        return bbuf.at[slot, half] if is_rhs(u) else buf.at[slot, u, half]

    home_slot = jnp.where(inner, 1 + a, 0)
    def load(u):
        return pltpu.make_async_copy(inputs[u].at[0], buf.at[home_slot, u], sem_home.at[u])

    def load_rhs(half, part):
        return pltpu.make_async_copy(
            b_ref.at[0, part, :, pl.ds(half * wide, wide)],
            bbuf.at[home_slot, half, :, pl.ds(part * wide, wide)],
            sem_bhome.at[half, part],
        )

    for u in (0, 1):
        load(u).start()
    for half in range(2):
        for part in range(2):
            load_rhs(half, part).start()

    barrier = pltpu.get_barrier_semaphore()

    def greet(who):
        pl.semaphore_signal(barrier, inc=1, device_id=who, device_id_type=MESH)

    greet(mate)
    greet(across)
    for exists, who in ((inner, twin), (has_far, far), (has_up2, up2), (has_down2, down2)):
        pl.when(exists)(functools.partial(greet, who))
    count = (
        2
        + inner.astype(jnp.int32)
        + has_far.astype(jnp.int32)
        + has_up2.astype(jnp.int32)
        + has_down2.astype(jnp.int32)
    )
    pl.semaphore_wait(barrier, count)

    def remote(src, dst, send, recv, who):
        return pltpu.make_async_remote_copy(
            src_ref=src, dst_ref=dst, send_sem=send, recv_sem=recv,
            device_id=who, device_id_type=MESH,
        )

    def send0(u, which, slot, who, half):
        return remote(
            bbuf.at[home_slot, half] if is_rhs(u) else inputs[u].at[0, half],
            place0(slot, u, half),
            sem_send0.at[which, u, half],
            sem_buf.at[slot, u, half],
            who,
        )

    def over_y(u, half):
        who = {"chain": jnp.where(inner, twin["chain"], across["chain"])}
        return send0(u, 0, jnp.where(inner, 0, 1 + a), who, half)

    def to_mate(u, half):
        return send0(u, 1, 2 - a, mate, half)

    def start_mate(u):
        for half in range(2):
            to_mate(u, half).start()

    def start_y(u):
        for half in range(2):
            over_y(u, half).start()

    @pl.when(inner)
    def _():
        start_mate(0)
        start_mate(1)

    @pl.when(a == 1)
    def _():
        start_y(0)
        start_y(1)

    @pl.when(a == 0)
    def _():
        start_y(1)
        start_y(0)

    for half in range(2):
        for part in range(2):
            load_rhs(half, part).wait()
    start_y(RHS)
    pl.when(inner)(lambda: start_mate(RHS))

    none_far0 = outer & jnp.logical_not(has_far)

    def clear(ref):
        ref[...] = jnp.zeros(ref.shape, ref.dtype)

    @pl.when(none_far0)
    def _():
        clear(buf.at[1 + a])
        clear(bbuf.at[1 + a])

    @pl.when(jnp.logical_not(has_down1))
    def _():
        clear(got1.at[0])
        clear(gb1.at[0])

    @pl.when(jnp.logical_not(has_up1))
    def _():
        clear(got1.at[1])
        clear(gb1.at[1])

    @pl.when(jnp.logical_not(has_down2))
    def _():
        clear(got2.at[0])
        clear(gb2.at[0])

    @pl.when(jnp.logical_not(has_up2))
    def _():
        clear(got2.at[1])
        clear(gb2.at[1])

    def arrive(ref, sem):
        pltpu.make_async_copy(ref, ref, sem).wait()

    for u in (0, 1):
        load(u).wait()

    def relay(u, half):
        return remote(
            place0(2 - a, u, half),
            place0(1 + a, u, half),
            sem_relay.at[u, half],
            sem_buf.at[1 + a, u, half],
            far,
        )

    def wait_half(u, half):
        arrive(place0(2 - a, u, half), sem_buf.at[2 - a, u, half])
        pl.when(inner & has_far)(lambda: relay(u, half).start())

    def wait_own(u, half):
        pl.when(inner)(lambda: arrive(place0(0, u, half), sem_buf.at[0, u, half]))

    def wait_unit(u):
        for half in range(2):
            wait_half(u, half)
        for half in range(2):
            wait_own(u, half)

    def wait_far(u, half):
        pl.when(outer & has_far)(
            lambda: arrive(place0(1 + a, u, half), sem_buf.at[1 + a, u, half])
        )

    row = lax.broadcasted_iota(jnp.int32, (l_ref.shape[2], l_ref.shape[3]), 0)
    col = lax.broadcasted_iota(jnp.int32, (l_ref.shape[2], l_ref.shape[3]), 1)
    unit = (row == col).astype(jnp.float32)

    def inverse(off):
        e1 = rounded(off)
        e2 = product(e1, e1)
        e2_low = rounded(e2)
        e3 = product(e1, e2_low)
        e4 = rounded(product(e2_low, e2_low))
        half_way = (unit + off[0] + e2[0] + e3[0], off[1] + e2[1] + e3[1])
        rest = product(rounded(half_way), e4)
        return rounded((half_way[0] + rest[0], half_way[1] + rest[1]))

    def negated(parts):
        return -parts[0], -parts[1]

    def coupled(one, two):
        return one[0] + two[0], one[1] + two[1]

    def by_rhs(left, right):
        order = left.shape[1]
        tall = left.reshape(2 * order, left.shape[2])
        both = jnp.dot(tall, right, preferred_element_type=jnp.float32)
        top, low = both[:order], both[order:]
        return jnp.concatenate(
            [top[:, :wide] - low[:, wide:], top[:, wide:] + low[:, :wide]], axis=1
        )

    def new_rhs(inv, own, one, two):
        return by_rhs(
            inv, (own.astype(jnp.float32) - one - two).astype(jnp.bfloat16)
        ).astype(jnp.bfloat16)

    def send1(u, to_up):
        side = 0 if to_up else 1
        rhs = is_rhs(u)
        return remote(
            nb1.at[u - RHS] if rhs else new1.at[u],
            gb1.at[side, u - RHS] if rhs else got1.at[side, u],
            sem_send1.at[side, u],
            sem_got1.at[side, u],
            up1 if to_up else down1,
        )

    def start1(u):
        pl.when(has_up1)(lambda: send1(u, True).start())
        pl.when(has_down1)(lambda: send1(u, False).start())

    wait_unit(f)
    mid[0] = rounded(negated(product(buf[0, f], buf[cf, f])))
    wait_unit(g)
    for half in range(2):
        wait_far(f, half)
    mid[2] = inverse(
        coupled(product(buf[0, f], buf[cf, g]), product(buf[0, g], buf[cg, f]))
    )
    new1[f] = rounded(product(mid[2], mid[0]))
    start1(f)
    for half in range(2):
        wait_far(g, half)
    mid[1] = rounded(negated(product(buf[0, g], buf[cg, g])))
    new1[g] = rounded(product(mid[2], mid[1]))
    start1(g)
    for half in range(2):
        wait_half(RHS, half)
    for half in range(2):
        wait_own(RHS, half)
        wait_far(RHS, half)
        one = by_rhs(buf[0, f], bbuf[cf, half])
        two = by_rhs(buf[0, g], bbuf[cg, half])
        nb1[half] = new_rhs(mid[2], bbuf[0, half], one, two)
        start1(RHS + half)

    def wait1(u):
        rhs = is_rhs(u)

        def one_side(side):
            arrive(gb1.at[side, u - RHS] if rhs else got1.at[side, u], sem_got1.at[side, u])

        pl.when(has_down1)(lambda: one_side(0))
        pl.when(has_up1)(lambda: one_side(1))

    def send2(place, to_up):
        side = 0 if to_up else 1
        return remote(
            new2.at[1 - side] if place == 0 else nb2.at[place - 1],
            got2.at[side] if place == 0 else gb2.at[side, place - 1],
            sem_send2.at[side, place],
            sem_got2.at[side, place],
            up2 if to_up else down2,
        )

    ef, eg = cf - 1, cg - 1
    wait1(f)
    mid[0] = rounded(negated(product(new1[f], got1[ef, f])))
    wait1(g)
    mid[2] = inverse(
        coupled(product(new1[f], got1[ef, g]), product(new1[g], got1[eg, f]))
    )
    new2[f] = rounded(product(mid[2], mid[0]))

    def start2(is_upper):
        pl.when(has_up2 & is_upper)(lambda: send2(0, True).start())
        pl.when(has_down2 & jnp.logical_not(is_upper))(lambda: send2(0, False).start())

    start2(f == 1)
    mid[1] = rounded(negated(product(new1[g], got1[eg, g])))
    new2[g] = rounded(product(mid[2], mid[1]))
    start2(g == 1)
    for half in range(2):
        wait1(RHS + half)
        one = by_rhs(new1[f], gb1[ef, half])
        two = by_rhs(new1[g], gb1[eg, half])
        nb2[half] = new_rhs(mid[2], nb1[half], one, two)
        pl.when(has_up2)(lambda half=half: send2(1 + half, True).start())
        pl.when(has_down2)(lambda half=half: send2(1 + half, False).start())

    def wait2(place):
        def one_side(side):
            arrive(got2.at[side] if place == 0 else gb2.at[side, place - 1], sem_got2.at[side, place])

        pl.when(has_down2)(lambda: one_side(0))
        pl.when(has_up2)(lambda: one_side(1))

    def spot(half, part):
        return (
            last.at[half, :, pl.ds(part * wide, wide)],
            out_ref.at[0, part, :, pl.ds(half * wide, wide)],
        )

    def home(half, part):
        src, dst = spot(half, part)
        return remote(src, dst, sem_out.at[0, half, part], sem_out.at[1, half, part], twin)

    def keep(half, part):
        src, dst = spot(half, part)
        return pltpu.make_async_copy(src, dst, sem_out.at[1, half, part])

    wait2(0)
    mid[2] = inverse(coupled(product(new2[0], got2[0]), product(new2[1], got2[1])))
    for half in range(2):
        wait2(1 + half)
        one = by_rhs(new2[0], gb2[0, half])
        two = by_rhs(new2[1], gb2[1, half])
        last[half] = new_rhs(mid[2], nb2[half], one, two)
        for part in range(2):
            pl.when(inner)(lambda half=half, part=part: home(half, part).start())
            pl.when(outer)(lambda half=half, part=part: keep(half, part).start())

    for u in range(3):
        for half in range(2):
            over_y(u, half).wait_send()
            pl.when(inner)(lambda u=u, half=half: to_mate(u, half).wait_send())
            pl.when(inner & has_far)(lambda u=u, half=half: relay(u, half).wait_send())
    for u in range(4):
        pl.when(has_up1)(lambda u=u: send1(u, True).wait_send())
        pl.when(has_down1)(lambda u=u: send1(u, False).wait_send())
    for place in range(3):
        pl.when(has_up2)(lambda place=place: send2(place, True).wait_send())
        pl.when(has_down2)(lambda place=place: send2(place, False).wait_send())
    for half in range(2):
        for part in range(2):
            pl.when(inner)(lambda half=half, part=part: home(half, part).wait())
            pl.when(outer)(lambda half=half, part=part: keep(half, part).wait())


def local(quads, lower, upper, right_side):
    block = lower.shape[1:]
    half = (right_side.shape[2], right_side.shape[3])
    any_spec = pl.BlockSpec(memory_space=pl.ANY)
    low = jnp.bfloat16
    dma = pltpu.SemaphoreType.DMA
    return pl.pallas_call(
        functools.partial(kernel, quads),
        out_shape=jax.ShapeDtypeStruct(right_side.shape, right_side.dtype),
        in_specs=[any_spec] * 3,
        out_specs=any_spec,
        scratch_shapes=[
            pltpu.VMEM((3, 2, *block), low),
            pltpu.VMEM((3, 2, *half), low),
            pltpu.VMEM((2, *block), low),
            pltpu.VMEM((2, *half), low),
            pltpu.VMEM((2, 2, *block), low),
            pltpu.VMEM((2, 2, *half), low),
            pltpu.VMEM((2, *block), low),
            pltpu.VMEM((2, *half), low),
            pltpu.VMEM((2, *block), low),
            pltpu.VMEM((2, 2, *half), low),
            pltpu.VMEM((2, *half), low),
            pltpu.VMEM((3, *block), low),
            dma((2,)),
            dma((2, 2)),
            dma((3, 3, 2)),
            dma((2, 3, 2)),
            dma((3, 2)),
            dma((2, 4)),
            dma((2, 4)),
            dma((2, 3)),
            dma((2, 3)),
            dma((2, 2, 2)),
        ],
        compiler_params=pltpu.CompilerParams(collective_id=0, has_side_effects=True),
    )(lower, upper, right_side)


def solution(mesh):
    placed = P(("energy", "chain"), None, None, None)
    return jax.shard_map(
        functools.partial(local, mesh.shape["chain"] // 4),
        mesh=mesh,
        in_specs=(placed,) * 3,
        out_specs=placed,
        check_vma=False,
    )
```

time: 57.6 us -> 53.8 us (0.934)
  the two profiles are of different devices: /device:TPU:11 before, /device:TPU:17 now
where the time goes in v2:
time: 53.8 us; the launch traced here: 53.7 us
  Pallas kernels  52 us (97%)
  local copies, waits for them, and re-layouts  1.67 us (3%)
    pallas_call x1, Pallas kernels, local(): pl.pallas_call(functools.partial(kernel, quads), out_shape=jax.ShapeDtype...  52 us
    unnamed x1, local copies, waits for them, and re-layouts  1.67 us

profile of v2, /device:TPU:17, one launch (start us, length us, event | category | flops | bytes accessed | tf_op | source)
XLA Modules:
  0.0 53.7 jit_solution(10677167051384113472)
XLA Ops:
  0.0 52.0 %shard_map.37 = bf16[1,2,256,256]{3,2,1,0:T(8,128)(2,1)} custom-call(bf16[1,2,256,256]{3,2,1,0:T(8,128)(2,1)} %l_ref.1, bf16[1,2,256,256]{3,2,1,0:T(8,128)(2,1)} %u_ref.1, bf16[1,2,256,256]{3,2,1,0:T(8,128)(2,1)} %b_ref.1), custom_call_target="tpu_custom_call" | custom-call | tf_op jit(solution)/shard_map/pallas_call | solution.py:388
  52.0 1.7 %copy.5 = bf16[1,2,256,256]{3,2,1,0:T(8,128)(2,1)} copy(bf16[1,2,256,256]{3,2,1,0:T(8,128)(2,1)} %shard_map.37) | data formatting | bytes 524288

commit v3 on v2

--- a/solution.py
+++ b/solution.py
@@ -30,9 +30,9 @@
 
 def kernel(
     quads, l_ref, u_ref, b_ref, out_ref,
-    buf, bbuf, new1, nb1, got1, gb1, new2, nb2, got2, gb2, last, mid,
+    buf, bbuf, new1, nb1, got1, gb1, new2, nb2, got2, gb2, last, mid, fwd,
     sem_home, sem_bhome, sem_buf, sem_send0, sem_relay,
-    sem_got1, sem_send1, sem_got2, sem_send2, sem_out,
+    sem_got1, sem_send1, sem_got2, sem_send2, sem_out, sem_fwd,
 ):
     me = lax.axis_index("chain")
     q = me // 4
@@ -57,6 +57,10 @@
     down2, has_down2 = at(q - 1, a, b), q >= 1
     far_step = 2 * b - 1
     far, has_far = at(q + far_step, a, 1 - b), (q + far_step >= 0) & (q + far_step < quads)
+    diag = at(q, 1 - a, 1 - b)
+    pass_on = {"chain": jnp.where(a == 0, down2["chain"], up2["chain"])}
+    has_far_in = ((a == 0) & has_up2) | ((a == 1) & has_down2)
+    has_pass_on = outer & (((a == 0) & has_down2) | ((a == 1) & has_up2))
     inputs = (l_ref, u_ref)
     wide = b_ref.shape[3] // 2
 
@@ -87,11 +91,10 @@
 
     greet(mate)
     greet(across)
-    for exists, who in ((inner, twin), (has_far, far), (has_up2, up2), (has_down2, down2)):
+    for exists, who in ((inner, twin), (outer, diag), (has_far, far), (has_up2, up2), (has_down2, down2)):
         pl.when(exists)(functools.partial(greet, who))
     count = (
-        2
-        + inner.astype(jnp.int32)
+        3
         + has_far.astype(jnp.int32)
         + has_up2.astype(jnp.int32)
         + has_down2.astype(jnp.int32)
@@ -149,6 +152,22 @@
     start_y(RHS)
     pl.when(inner)(lambda: start_mate(RHS))
 
+    def hand_on(half):
+        return remote(
+            bbuf.at[0, half], fwd.at[half], sem_fwd.at[0, half], sem_fwd.at[1, half], pass_on
+        )
+
+    def hand_across(half):
+        return remote(
+            fwd.at[half], bbuf.at[2 - a, half], sem_fwd.at[2, half],
+            sem_buf.at[2 - a, RHS, half], diag,
+        )
+
+    @pl.when(has_pass_on)
+    def _():
+        for half in range(2):
+            hand_on(half).start()
+
     none_far0 = outer & jnp.logical_not(has_far)
 
     def clear(ref):
@@ -196,7 +215,8 @@
 
     def wait_half(u, half):
         arrive(place0(2 - a, u, half), sem_buf.at[2 - a, u, half])
-        pl.when(inner & has_far)(lambda: relay(u, half).start())
+        if not is_rhs(u):
+            pl.when(inner & has_far)(lambda: relay(u, half).start())
 
     def wait_own(u, half):
         pl.when(inner)(lambda: arrive(place0(0, u, half), sem_buf.at[0, u, half]))
@@ -217,14 +237,13 @@
     unit = (row == col).astype(jnp.float32)
 
     def inverse(off):
-        e1 = rounded(off)
-        e2 = product(e1, e1)
-        e2_low = rounded(e2)
-        e3 = product(e1, e2_low)
-        e4 = rounded(product(e2_low, e2_low))
-        half_way = (unit + off[0] + e2[0] + e3[0], off[1] + e2[1] + e3[1])
-        rest = product(rounded(half_way), e4)
-        return rounded((half_way[0] + rest[0], half_way[1] + rest[1]))
+        low = rounded((unit - off[0], -off[1]))
+        approx = rounded((unit + off[0], off[1]))
+        for _ in range(2):
+            prod = product(low, approx)
+            fix = rounded((2.0 * unit - prod[0], -prod[1]))
+            approx = rounded(product(approx, fix))
+        return approx
 
     def negated(parts):
         return -parts[0], -parts[1]
@@ -263,6 +282,13 @@
 
     wait_unit(f)
     mid[0] = rounded(negated(product(buf[0, f], buf[cf, f])))
+
+    @pl.when(outer & has_far_in)
+    def _():
+        for half in range(2):
+            arrive(fwd.at[half], sem_fwd.at[1, half])
+            hand_across(half).start()
+
     wait_unit(g)
     for half in range(2):
         wait_far(f, half)
@@ -366,7 +392,11 @@
         for half in range(2):
             over_y(u, half).wait_send()
             pl.when(inner)(lambda u=u, half=half: to_mate(u, half).wait_send())
-            pl.when(inner & has_far)(lambda u=u, half=half: relay(u, half).wait_send())
+            if u != RHS:
+                pl.when(inner & has_far)(lambda u=u, half=half: relay(u, half).wait_send())
+    for half in range(2):
+        pl.when(has_pass_on)(lambda half=half: hand_on(half).wait_send())
+        pl.when(outer & has_far_in)(lambda half=half: hand_across(half).wait_send())
     for u in range(4):
         pl.when(has_up1)(lambda u=u: send1(u, True).wait_send())
         pl.when(has_down1)(lambda u=u: send1(u, False).wait_send())
@@ -403,6 +433,7 @@
             pltpu.VMEM((2, 2, *half), low),
             pltpu.VMEM((2, *half), low),
             pltpu.VMEM((3, *block), low),
+            pltpu.VMEM((2, *half), low),
             dma((2,)),
             dma((2, 2)),
             dma((3, 3, 2)),
@@ -413,6 +444,7 @@
             dma((2, 3)),
             dma((2, 3)),
             dma((2, 2, 2)),
+            dma((3, 2)),
         ],
         compiler_params=pltpu.CompilerParams(collective_id=0, has_side_effects=True),
     )(lower, upper, right_side)

time: 53.8 us -> 53.1 us (0.987)
  the two profiles are of different devices: /device:TPU:17 before, /device:TPU:11 now
where the time goes in v3:
time: 53.1 us; the launch traced here: 53 us
  Pallas kernels  51.3 us (97%)
  local copies, waits for them, and re-layouts  1.67 us (3%)
    pallas_call x1, Pallas kernels, local(): pl.pallas_call(functools.partial(kernel, quads), out_shape=jax.ShapeDtype...  51.3 us
    unnamed x1, local copies, waits for them, and re-layouts  1.67 us

profile of v3, /device:TPU:11, one launch (start us, length us, event | category | flops | bytes accessed | tf_op | source)
XLA Modules:
  0.0 53.0 jit_solution(17292163760593185847)
XLA Ops:
  0.0 51.3 %shard_map.37 = bf16[1,2,256,256]{3,2,1,0:T(8,128)(2,1)} custom-call(bf16[1,2,256,256]{3,2,1,0:T(8,128)(2,1)} %l_ref.1, bf16[1,2,256,256]{3,2,1,0:T(8,128)(2,1)} %u_ref.1, bf16[1,2,256,256]{3,2,1,0:T(8,128)(2,1)} %b_ref.1), custom_call_target="tpu_custom_call" | custom-call | tf_op jit(solution)/shard_map/pallas_call | solution.py:418
  51.3 1.7 %copy.5 = bf16[1,2,256,256]{3,2,1,0:T(8,128)(2,1)} copy(bf16[1,2,256,256]{3,2,1,0:T(8,128)(2,1)} %shard_map.37) | data formatting | bytes 524288

commit v4 on v3

--- a/solution.py
+++ b/solution.py
@@ -304,7 +304,6 @@
     start1(g)
     for half in range(2):
         wait_half(RHS, half)
-    for half in range(2):
         wait_own(RHS, half)
         wait_far(RHS, half)
         one = by_rhs(buf[0, f], bbuf[cf, half])

time: 53.1 us -> 53.1 us (level)
  no operation moved by 1% of the time
where the time goes in v4:
time: 53.1 us; the launch traced here: 53 us
  Pallas kernels  51.3 us (97%)
  local copies, waits for them, and re-layouts  1.67 us (3%)
    pallas_call x1, Pallas kernels, local(): pl.pallas_call(functools.partial(kernel, quads), out_shape=jax.ShapeDtype...  51.3 us
    unnamed x1, local copies, waits for them, and re-layouts  1.67 us

profile of v4, /device:TPU:11, one launch (start us, length us, event | category | flops | bytes accessed | tf_op | source)
XLA Modules:
  0.0 53.0 jit_solution(16430752991388349735)
XLA Ops:
  0.0 51.3 %shard_map.37 = bf16[1,2,256,256]{3,2,1,0:T(8,128)(2,1)} custom-call(bf16[1,2,256,256]{3,2,1,0:T(8,128)(2,1)} %l_ref.1, bf16[1,2,256,256]{3,2,1,0:T(8,128)(2,1)} %u_ref.1, bf16[1,2,256,256]{3,2,1,0:T(8,128)(2,1)} %b_ref.1), custom_call_target="tpu_custom_call" | custom-call | tf_op jit(solution)/shard_map/pallas_call | solution.py:417
  51.3 1.7 %copy.5 = bf16[1,2,256,256]{3,2,1,0:T(8,128)(2,1)} copy(bf16[1,2,256,256]{3,2,1,0:T(8,128)(2,1)} %shard_map.37) | data formatting | bytes 524288
